TPU v7x, 128 devices: a whole 4x4x4 slice. The times are simulated.
128 devices in a mesh: seq: 16 (over x_lo, z, core), tp: 8 (over y, x_hi).
Axes of the slice: x: 4 (x_hi: 2, x_lo: 2; x = x_hi * 2 + x_lo), y: 4, z: 4, core: 2. Of those that a mesh axis runs over, the one named last changes fastest.
Arguments:
- hidden_in: bfloat16 [6144, 3584], P('seq'), may hold values from -48 to 48
- joined_inputs: bfloat16 [6144, 8192], P('seq', 'tp'), may hold values from -64 to 64
- lengths: int32 [4], replicated, may hold values from 1 to 3072, 6144 in all
- o_weight: bfloat16 [4096, 3584], P('tp'), may hold values from -0.09375 to 0.09375
- gate_up: float32 [2, 3584, 7168], P(None, ('seq', 'tp')), may hold values from -0.09375 to 0.09375
- down_weight: bfloat16 [7168, 3584], P('tp'), may hold values from -0.0625 to 0.0625
- next_weight: bfloat16 [3584, 8192], P(None, 'tp'), may hold values from -0.09375 to 0.09375
- post_attn_gain: float32 [3584], replicated, may hold values from 0.1 to 1.9
- pre_ffw_gain: float32 [3584], replicated, may hold values from 0.1 to 1.9
- post_ffw_gain: float32 [3584], replicated, may hold values from 0.1 to 1.9
- next_gain: float32 [3584], replicated, may hold values from 0.1 to 1.9
Outputs:
- next_qkv: bfloat16 [6144, 8192], P('seq', 'tp')
Inputs may be any that keep to these rules, and one draw needn't show every extreme that they name: The lengths of 4 prompts laid end to end; they sum to 6144 and the longest is exactly 3072.
All inputs are finite; a program needn't handle non-finite values.
Results may differ from a plain program's by a relative error of at most 0.022.
Values may be sent and summed in bfloat16 or wider, within the bound.
A program may use at most 192 MiB of HBM per device.

v0:
```python
import jax
import jax.numpy as jnp
from jax import lax
from jax.sharding import PartitionSpec as P

HEADS = 16
KV_HEADS = 8
HEAD_DIM = 256


def rms_norm(values, gain):
    meansq = jnp.mean(values * values, axis=-1, keepdims=True)
    return values * lax.rsqrt(meansq + 1e-06) * gain


def local(
    hidden_in,
    joined_inputs,
    lengths,
    o_weight,
    gate_up,
    down_weight,
    next_weight,
    post_attn_gain,
    pre_ffw_gain,
    post_ffw_gain,
    next_gain,
):
    tp_count = lax.axis_size("tp")
    row_count = hidden_in.shape[0]
    per_group = HEADS // KV_HEADS
    group_cols = (per_group + 2) * HEAD_DIM
    local_groups = joined_inputs.shape[1] // group_cols
    grouped = joined_inputs.reshape(row_count, local_groups, group_cols)
    queries = grouped[:, :, : per_group * HEAD_DIM].reshape(
        row_count, local_groups, per_group, HEAD_DIM
    )
    own_keys = grouped[:, :, per_group * HEAD_DIM : (per_group + 1) * HEAD_DIM]
    own_values = grouped[:, :, (per_group + 1) * HEAD_DIM :]
    keys_all, values_all = (
        lax.all_gather(own_keys, "seq", axis=0, tiled=True),
        lax.all_gather(own_values, "seq", axis=0, tiled=True),
    )
    total_rows = keys_all.shape[0]
    seq_index = lax.axis_index("seq")
    position = seq_index * row_count
    ends = jnp.cumsum(lengths)
    places = jnp.arange(total_rows, dtype=jnp.int32)
    prompt_ids = jnp.sum((places[:, None] >= ends[None, :]).astype(jnp.int32), axis=1)
    query_place = position + jnp.arange(row_count, dtype=jnp.int32)
    query_ids = lax.dynamic_slice_in_dim(prompt_ids, position, row_count, 0)
    scale = HEAD_DIM ** (-0.5)
    scores = (
        jnp.einsum("qgrd,kgd->qgrk", queries, keys_all, preferred_element_type=jnp.float32) * scale
    )
    allowed = (
        (query_ids[:, None] == prompt_ids[None, :]) & (places[None, :] <= query_place[:, None])
    )[:, None, None, :]
    scores = jnp.where(allowed, scores, -jnp.inf)
    peak = jnp.max(scores, axis=-1, keepdims=True)
    weights = jnp.where(allowed, jnp.exp(scores - peak), 0.0)
    norm_sum = jnp.sum(weights, axis=-1)
    blended = jnp.einsum(
        "qgrk,kgd->qgrd",
        weights.astype(jnp.bfloat16),
        values_all,
        preferred_element_type=jnp.float32,
    )
    blended = blended / norm_sum[..., None]
    attended = blended.astype(jnp.bfloat16).reshape(row_count, local_groups * per_group * HEAD_DIM)
    projected = jnp.dot(attended, o_weight, preferred_element_type=jnp.float32)
    tp_index = lax.axis_index("tp")
    slice_rows = row_count // tp_count

    def scattered(values):
        return lax.psum_scatter(
            values.astype(jnp.bfloat16), "tp", scatter_dimension=0, tiled=True
        ).astype(jnp.float32)

    own_hidden = lax.dynamic_slice_in_dim(hidden_in, tp_index * slice_rows, slice_rows, 0)
    residual_mid = own_hidden.astype(jnp.float32) + rms_norm(scattered(projected), post_attn_gain)
    ffw_in = rms_norm(residual_mid, pre_ffw_gain).astype(jnp.bfloat16)
    ffw_in = lax.all_gather(ffw_in, "tp", axis=0, tiled=True)
    server_low = gate_up.astype(jnp.bfloat16)
    unit_rows = lax.all_to_all(server_low, "tp", split_axis=2, concat_axis=1, tiled=True)
    local_units = lax.all_gather(unit_rows, "seq", axis=1, tiled=True)
    gate = jnp.dot(ffw_in, local_units[0], preferred_element_type=jnp.float32)
    up_part = jnp.dot(ffw_in, local_units[1], preferred_element_type=jnp.float32)
    activated = (jax.nn.gelu(gate, approximate=True) * up_part).astype(jnp.bfloat16)
    ffw_out = jnp.dot(activated, down_weight, preferred_element_type=jnp.float32)
    residual_out = residual_mid + rms_norm(scattered(ffw_out), post_ffw_gain)
    next_in = rms_norm(residual_out, next_gain).astype(jnp.bfloat16)
    next_in = lax.all_gather(next_in, "tp", axis=0, tiled=True)
    return jnp.dot(next_in, next_weight, preferred_element_type=jnp.float32).astype(jnp.bfloat16)


def solution(mesh):
    in_specs = (
        P("seq", None),
        P("seq", "tp"),
        P(),
        P("tp", None),
        P(None, ("seq", "tp"), None),
        P("tp", None),
        P(None, "tp"),
        P(),
        P(),
        P(),
        P(),
    )
    out_specs = P("seq", "tp")
    return jax.shard_map(local, mesh=mesh, in_specs=in_specs, out_specs=out_specs, check_vma=False)
```

profile of v0, /device:TPU:1, one launch (start us, length us, event | category | flops | bytes accessed | tf_op | source)
XLA Modules:
  0.0 497.7 jit_solution(12675945497495161882)
XLA Ops:
  6.5 0.0 all-gather.6.cloned.1.call-start
  6.5 1.8 fusion.47
  8.3 0.0 all-gather.6.cloned.1.call-update
  8.3 0.0 all-gather.8.cloned.1.call-start
  8.4 0.7 all-gather.8.cloned.1.call-update
  9.1 0.0 reduce-scatter.3.cloned.1.call-start
  9.1 1.0 slice.21
  10.2 0.8 reduce-window.8
  11.0 0.2 copy.48
  11.2 0.1 convert_reduce_fusion
  11.4 0.1 dynamic_slice.7
  11.5 3.8 fusion.6
  15.2 33.6 %all-gather.6.cloned.1.call-done = bf16[6144,1,256]{2,0,1:T(8,128)(2,1)} async-done(((bf16[384,1,256]{2,0,1:T(8,128)(2,1)}), bf16[6144,1,256]{2,0,1:T(8,128)(2,1)}) %all-gather.6.cloned.1.call-update) | async-done | bytes 3145744 | tf_op jit(solution)/shard_map/all_gather | solution.py:41
  48.8 5.4 %fusion = (f32[384,2]{0,1:T(2,128)S(1)}, f32[6144,384,2]{1,0,2:T(8,128)S(1)}) fusion(pred[384,6144]{0,1:T(8,128)(4,1)} %fusion.6, bf16[384,2,256]{0,2,1:T(8,128)(2,1)S(1)} %bitcast.100, bf16[6144,1,256]{2,0,1:T(8,128)(2,1)} %all-gather.6.cloned.1.call-done), kind=kOutput, calls=%fused_computation.2 | convolution fusion | flops 2430074112 | bytes 24775680 | tf_op jit(solution)/shard_map/qgrd,kgd->qgrk/dot_general | solution.py:54
  54.2 0.0 copy-start
  54.2 6.4 %copy-done = f32[6144,384,2]{1,0,2:T(8,128)} copy-done((f32[6144,384,2]{1,0,2:T(8,128)}, f32[6144,384,2]{1,0,2:T(8,128)S(1)}, u32[]{:S(2)}) %copy-start) | copy-done | bytes 18874392
  60.6 6.1 %fusion.1 = f32[384,2]{0,1:T(2,128)S(1)} fusion(f32[6144,384,2]{1,0,2:T(8,128)S(1)} %get-tuple-element.10, f32[384,2]{0,1:T(2,128)S(1)} %get-tuple-element.9, pred[384,6144]{0,1:T(8,128)(4,1)} %fusion.6), kind=kLoop, calls=%fused_computation.3 | loop fusion | flops 23592192 | bytes 21239808 | tf_op jit(solution)/shard_map/reduce_sum | solution.py:62
  66.8 19.7 %all-gather.8.cloned.1.call-done = bf16[6144,1,256]{2,0,1:T(8,128)(2,1)} async-done(((bf16[384,1,256]{2,0,1:T(8,128)(2,1)}), bf16[6144,1,256]{2,0,1:T(8,128)(2,1)}) %all-gather.8.cloned.1.call-update) | async-done | bytes 3145744 | tf_op jit(solution)/shard_map/all_gather | solution.py:42
  86.5 0.0 copy-start.2
  86.5 13.2 %fusion.32 = bf16[1,256,384,2]{2,1,3,0:T(8,128)(2,1)S(1)} fusion(bf16[6144,1,256]{2,0,1:T(8,128)(2,1)} %all-gather.8.cloned.1.call-done, f32[6144,384,2]{1,0,2:T(8,128)} %copy-done, f32[384,2]{0,1:T(2,128)S(1)} %get-tuple-element.9, pred[384,6144]{0,1:T(8,128)(4,1)} %fusion.6, f32[384,2]{0,1:T(2,128)S(1)} %fusion.1), kind=kOutput, calls=%fused_computation.33 | convolution fusion | flops 2439905280 | bytes 24778752 | tf_op jit(solution)/shard_map/qgrk,kgd->qgrd/dot_general | solution.py:63
  99.7 0.0 copy-done.2
  99.7 0.0 copy-start.3
  99.7 3.2 convolution_convert_fusion
  102.8 0.0 reduce-scatter.3.cloned.1.call-update
  102.9 0.2 all-gather.12.cloned.1.call-start
  103.1 0.0 copy-done.3
  103.1 0.5 copy.72
  103.6 6.2 %copy.53 = bf16[2,28,7168]{1,0,2:T(2,128)(2,1)} copy(bf16[2,28,7168]{2,1,0:T(8,128)(2,1)S(1)} %copy.72) | data formatting | bytes 1605632 | tf_op jit(solution)/shard_map/convert_element_type | solution.py:84
  109.8 8.3 %reshape.151 = bf16[8,2,25088]{2,1,0:T(2,128)(2,1)S(1)} reshape(bf16[7168,2,28]{2,1,0:T(2,128)(2,1)} %bitcast.95) | data formatting | bytes 1605632
  118.0 21.5 %all_to_all.18 = bf16[8,2,25088]{2,1,0:T(2,128)(2,1)S(1)} all-to-all(bf16[8,2,25088]{2,1,0:T(2,128)(2,1)S(1)} %reshape.151), channel_id=1, replica_groups=mesh['seq'=16,'tp'=8] {'tp'}, dimensions={0} | all-to-all | bytes 1605632 | tf_op jit(solution)/shard_map/all_to_all | solution.py:85
  139.5 10.6 %reshape.152 = bf16[7168,2,28]{2,1,0:T(2,128)(2,1)} reshape(bf16[8,2,25088]{2,1,0:T(2,128)(2,1)S(1)} %all_to_all.18) | data formatting | bytes 1605632
  150.1 0.0 copy-start.4
  150.1 0.0 copy-start.5
  150.1 9.9 %copy.54 = bf16[2,28,8,896]{3,0,1,2:T(2,128)(2,1)} copy(bf16[2,28,8,896]{1,0,3,2:T(2,128)(2,1)} %bitcast.96) | data formatting | bytes 1605632 | tf_op jit(solution)/shard_map/all_to_all | solution.py:85
  160.0 0.0 all-gather.12.cloned.1.call-update
  160.0 0.0 all-gather.10.cloned.1.call-start
  160.1 22.6 %reduce-scatter.3.cloned.1.call-done = bf16[48,3584]{1,0:T(8,128)(2,1)} async-done(((bf16[384,3584]{1,0:T(8,128)(2,1)}), bf16[48,3584]{1,0:T(8,128)(2,1)}) %reduce-scatter.3.cloned.1.call-update) | async-done | bytes 344080 | tf_op jit(solution)/shard_map/reduce_scatter | solution.py:76
  182.7 1.1 fusion.37
  183.9 0.0 copy-done.4
  183.9 0.0 copy-done.5
  183.9 1.3 multiply_reduce_fusion.1
  185.2 0.0 copy-done.7
  185.2 1.9 multiply_convert_fusion.1
  187.2 0.0 all-gather.10.cloned.1.call-update
  187.2 0.0 reduce-scatter.5.cloned.1.call-start
  187.2 70.7 %all-gather.12.cloned.1.call-done = bf16[2,3584,896]{2,0,1:T(2,128)(2,1)} async-done(((bf16[2,224,896]{2,0,1:T(2,128)(2,1)}), bf16[2,3584,896]{2,0,1:T(2,128)(2,1)}) %all-gather.12.cloned.1.call-update) | async-done | bytes 12845072 | tf_op jit(solution)/shard_map/all_gather | solution.py:86
  258.0 26.0 %fusion.46 = (bf16[1,3584,896]{2,0,1:T(2,128)(2,1)}, bf16[1,3584,896]{2,0,1:T(2,128)(2,1)}) fusion(bf16[2,3584,896]{2,0,1:T(2,128)(2,1)} %all-gather.12.cloned.1.call-done), kind=kLoop, calls=%fused_computation.58 | loop fusion | bytes 25690112 | tf_op jit(solution)/shard_map/slice | solution.py:87
  284.0 35.7 %all-gather.10.cloned.1.call-done = bf16[384,3584]{1,0:T(8,128)(2,1)} async-done(((bf16[48,3584]{1,0:T(8,128)(2,1)}), bf16[384,3584]{1,0:T(8,128)(2,1)}) %all-gather.10.cloned.1.call-update) | async-done | bytes 2752528 | tf_op jit(solution)/shard_map/all_gather | solution.py:83
  319.7 9.6 %fusion.9 = f32[384,896]{1,0:T(8,128)} fusion(bf16[384,3584]{1,0:T(8,128)(2,1)} %all-gather.10.cloned.1.call-done, bf16[1,3584,896]{2,0,1:T(2,128)(2,1)} %get-tuple-element.5), kind=kOutput, calls=%fused_computation.13 | convolution fusion | flops 2466250752 | bytes 10551296 | tf_op jit(solution)/shard_map/dot_general | solution.py:87
  329.3 0.0 copy-start.1
  329.3 0.0 copy-start.6
  329.3 15.2 %convolution_convert_fusion.1 = bf16[384,3584]{1,0:T(8,128)(2,1)} fusion(bf16[896,3584]{1,0:T(8,128)(2,1)} %param.16, bf16[384,3584]{1,0:T(8,128)(2,1)} %all-gather.10.cloned.1.call-done, bf16[1,3584,896]{2,0,1:T(2,128)(2,1)} %get-tuple-element.6, f32[384,896]{1,0:T(8,128)} %fusion.9), kind=kOutput, calls=%fused_computation.15 | convolution fusion | flops 4937318400 | bytes 19726336 | tf_op jit(solution)/shard_map/dot_general | solution.py:90
  344.5 0.0 reduce-scatter.5.cloned.1.call-update
  344.5 0.3 all-gather.14.cloned.1.call-start
  344.8 74.3 %reduce-scatter.5.cloned.1.call-done = bf16[48,3584]{1,0:T(8,128)(2,1)} async-done(((bf16[384,3584]{1,0:T(8,128)(2,1)}), bf16[48,3584]{1,0:T(8,128)(2,1)}) %reduce-scatter.5.cloned.1.call-update) | async-done | bytes 344080 | tf_op jit(solution)/shard_map/reduce_scatter | solution.py:76
  419.1 1.1 fusion.40
  420.3 0.0 copy-done.1
  420.3 0.0 copy-done.6
  420.3 1.4 multiply_reduce_fusion
  421.7 0.0 copy-done.8
  421.7 2.0 multiply_convert_fusion
  423.8 0.0 all-gather.14.cloned.1.call-update
  423.8 59.3 %all-gather.14.cloned.1.call-done = bf16[384,3584]{1,0:T(8,128)(2,1)} async-done(((bf16[48,3584]{1,0:T(8,128)(2,1)}), bf16[384,3584]{1,0:T(8,128)(2,1)}) %all-gather.14.cloned.1.call-update) | async-done | bytes 2752528 | tf_op jit(solution)/shard_map/all_gather | solution.py:93
  483.1 7.8 %convolution_convert_fusion.2 = bf16[384,1024]{1,0:T(8,128)(2,1)} fusion(bf16[384,3584]{1,0:T(8,128)(2,1)} %all-gather.14.cloned.1.call-done, bf16[3584,1024]{1,0:T(8,128)(2,1)} %param.17), kind=kOutput, calls=%fused_computation.22 | convolution fusion | flops 2818965504 | bytes 10878976 | tf_op jit(solution)/shard_map/dot_general | solution.py:94
  (7 shorter events, 0.0 us)
Async XLA Ops:
  6.5 42.2 %all-gather.6.cloned.1.call-start = ((), (), s32[]{:S(2)}) async-start(), calls=%async_computation.3 | async-start | bytes 3342336 | tf_op jit(solution)/shard_map/all_gather | solution.py:41
  8.3 78.1 %all-gather.8.cloned.1.call-start = ((), (), s32[]{:S(2)}) async-start(), calls=%async_computation.4 | async-start | bytes 3342336 | tf_op jit(solution)/shard_map/all_gather | solution.py:42
  9.1 173.6 %reduce-scatter.3.cloned.1.call-start = ((), (), s32[]{:S(2)}) async-start(), calls=%async_computation.5 | async-start | bytes 3096576 | tf_op jit(solution)/shard_map/reduce_scatter | solution.py:76
  54.2 6.5 %copy-start = (f32[6144,384,2]{1,0,2:T(8,128)}, f32[6144,384,2]{1,0,2:T(8,128)S(1)}, u32[]{:S(2)}) copy-start(f32[6144,384,2]{1,0,2:T(8,128)S(1)} %get-tuple-element.10) | copy-start | bytes 56623108
  86.5 13.2 %copy-start.2 = (bf16[512,3584]{1,0:T(8,128)(2,1)S(1)}, bf16[512,3584]{1,0:T(8,128)(2,1)}, u32[]{:S(2)}) copy-start(bf16[512,3584]{1,0:T(8,128)(2,1)} %param.14) | copy-start | bytes 11010052
  99.7 3.4 copy-start.3
  102.9 155.1 %all-gather.12.cloned.1.call-start = ((), (), s32[]{:S(2)}) async-start(), calls=%async_computation.7 | async-start | bytes 13647872 | tf_op jit(solution)/shard_map/all_gather | solution.py:86
  150.1 33.8 %copy-start.4 = (bf16[384,3584]{1,0:T(8,128)(2,1)S(1)}, bf16[384,3584]{1,0:T(8,128)(2,1)}, u32[]{:S(2)}) copy-start(bf16[384,3584]{1,0:T(8,128)(2,1)} %param.11) | copy-start | bytes 8257540
  150.1 33.8 %copy-start.5 = (f32[3584]{0:T(1024)S(1)}, f32[3584]{0:T(1024)}, u32[]{:S(2)}) copy-start(f32[3584]{0:T(1024)} %param.18) | copy-start | bytes 43012
  150.1 35.1 %copy-start.7 = (f32[3584]{0:T(1024)S(1)}, f32[3584]{0:T(1024)}, u32[]{:S(2)}) copy-start(f32[3584]{0:T(1024)} %param.19) | copy-start | bytes 43012
  160.0 159.7 %all-gather.10.cloned.1.call-start = ((), (), s32[]{:S(2)}) async-start(), calls=%async_computation.6 | async-start | bytes 3096576 | tf_op jit(solution)/shard_map/all_gather | solution.py:83
  187.2 231.9 %reduce-scatter.5.cloned.1.call-start = ((), (), s32[]{:S(2)}) async-start(), calls=%async_computation.8 | async-start | bytes 3096576 | tf_op jit(solution)/shard_map/reduce_scatter | solution.py:76
  329.3 91.0 %copy-start.1 = (bf16[48,3584]{1,0:T(8,128)(2,1)S(1)}, bf16[48,3584]{1,0:T(8,128)(2,1)}, u32[]{:S(2)}) copy-start(bf16[48,3584]{1,0:T(8,128)(2,1)} %reduce-scatter.3.cloned.1.call-done) | copy-start | bytes 1032196
  329.3 91.0 %copy-start.6 = (f32[3584]{0:T(1024)S(1)}, f32[3584]{0:T(1024)}, u32[]{:S(2)}) copy-start(f32[3584]{0:T(1024)} %param.20) | copy-start | bytes 43012
  344.5 77.2 %copy-start.8 = (f32[3584]{0:T(1024)S(1)}, f32[3584]{0:T(1024)}, u32[]{:S(2)}) copy-start(f32[3584]{0:T(1024)} %param.21) | copy-start | bytes 43012
  344.5 138.5 %all-gather.14.cloned.1.call-start = ((), (), s32[]{:S(2)}) async-start(), calls=%async_computation.9 | async-start | bytes 3096576 | tf_op jit(solution)/shard_map/all_gather | solution.py:93
Sparse Core Ops, SparseCore 0:
  9.1 39.6 all-gather.5
  50.5 35.9 all-gather.7
  103.0 79.6 reduce-scatter.2
  184.3 73.6 all-gather.11
  260.1 59.5 all-gather.9
  344.6 74.4 reduce-scatter.4
  423.9 59.1 all-gather.13
where the time goes:
time: 498 us
  waiting for transfers between devices  317 us (64%)
  local copies, waits for them, and re-layouts  71 us (14%)
  matrix products  54.3 us (11%)
  blocking collectives  21.5 us (4%)
  other arithmetic  19.9 us (4%)
  between operations  13.7 us (3%)
    reduce_scatter x2, waiting for transfers between devices, scattered(): lax.psum_scatter(values.astype(jnp.bfloat16), 'tp', scatter_dimension=0,...  96.9 us
    all_gather x1, waiting for transfers between devices, local(): local_units = lax.all_gather(unit_rows, 'seq', axis=1, tiled=True)  70.7 us
    all_gather x1, waiting for transfers between devices, local(): next_in = lax.all_gather(next_in, 'tp', axis=0, tiled=True)  59.3 us
    all_gather x1, waiting for transfers between devices, local(): ffw_in = lax.all_gather(ffw_in, 'tp', axis=0, tiled=True)  35.7 us
    all_gather x1, waiting for transfers between devices, local(): lax.all_gather(own_keys, 'seq', axis=0, tiled=True)  33.6 us
    slice x1, local copies, waits for them, and re-layouts, local(): gate = jnp.dot(ffw_in, local_units[0], preferred_element_type=jnp.float32)  26 us
    unnamed x21, local copies, waits for them, and re-layouts  25.8 us
    all_to_all x1, blocking collectives, local(): lax.all_to_all(server_low, 'tp', split_axis=2, concat_axis=1, tiled=True)  21.5 us
  transfers between devices with their start and end apart: 7, of which 7 were waited for; matrix products, arithmetic and copies ran while one was open for 17% of the time, Pallas kernels for 0%

commit v1 on v0

--- a/solution.py
+++ b/solution.py
@@ -90,7 +90,9 @@
     ffw_out = jnp.dot(activated, down_weight, preferred_element_type=jnp.float32)
     residual_out = residual_mid + rms_norm(scattered(ffw_out), post_ffw_gain)
     next_in = rms_norm(residual_out, next_gain).astype(jnp.bfloat16)
-    next_in = lax.all_gather(next_in, "tp", axis=0, tiled=True)
+    next_in = jnp.concatenate(
+        lax.all_to_all(jnp.stack([next_in] * lax.axis_size("tp")), "tp", 0, 0), axis=0
+    )
     return jnp.dot(next_in, next_weight, preferred_element_type=jnp.float32).astype(jnp.bfloat16)
 
 

time: 498 us -> 476 us (0.956)
  waiting for transfers between devices: 317 us -> 258 us
  blocking collectives: 21.5 us -> 57.6 us
    all_gather x1 -> x0, waiting for transfers between devices: 59.3 us -> none  [local(): next_in = lax.all_gather(next_in, 'tp', axis=0, tiled=True)]
    all_to_all x0 -> x1, blocking collectives: none -> 36.1 us  [local(): lax.all_to_all(jnp.stack([next_in] * lax.axis_size('tp')), 'tp', 0, 0)]
  transfers between devices with their start and end apart: 7 -> 6, of which waited for: 7 -> 6; matrix products, arithmetic and copies ran while one was open for 17% -> 18% of each run, Pallas kernels for 0% -> 0%
where the time goes in v1:
time: 476 us; the launch traced here: 473 us
  waiting for transfers between devices  258 us (54%)
  local copies, waits for them, and re-layouts  71.2 us (15%)
  blocking collectives  57.6 us (12%)
  matrix products  53.6 us (11%)
  other arithmetic  19.2 us (4%)
  between operations  13.7 us (3%)
    reduce_scatter x2, waiting for transfers between devices, scattered(): lax.psum_scatter(values.astype(jnp.bfloat16), 'tp', scatter_dimension=0,...  97.2 us
    all_gather x1, waiting for transfers between devices, local(): local_units = lax.all_gather(unit_rows, 'seq', axis=1, tiled=True)  70.7 us
    all_to_all x1, blocking collectives, local(): lax.all_to_all(jnp.stack([next_in] * lax.axis_size('tp')), 'tp', 0, 0)  36.1 us
    all_gather x1, waiting for transfers between devices, local(): ffw_in = lax.all_gather(ffw_in, 'tp', axis=0, tiled=True)  35.7 us
    all_gather x1, waiting for transfers between devices, local(): lax.all_gather(own_keys, 'seq', axis=0, tiled=True)  33.6 us
    slice x1, local copies, waits for them, and re-layouts, local(): gate = jnp.dot(ffw_in, local_units[0], preferred_element_type=jnp.float32)  26 us
    unnamed x21, local copies, waits for them, and re-layouts  25.8 us
    all_to_all x1, blocking collectives, local(): lax.all_to_all(server_low, 'tp', split_axis=2, concat_axis=1, tiled=True)  21.5 us
  transfers between devices with their start and end apart: 6, of which 6 were waited for; matrix products, arithmetic and copies ran while one was open for 18% of the time, Pallas kernels for 0%

profile of v1, /device:TPU:1, one launch (start us, length us, event | category | flops | bytes accessed | tf_op | source)
XLA Modules:
  0.0 473.3 jit_solution(14009299254812418653)
XLA Ops:
  6.5 0.0 all-gather.5.cloned.1.call-start
  6.5 1.8 fusion.47
  8.3 0.0 all-gather.5.cloned.1.call-update
  8.3 0.0 all-gather.7.cloned.1.call-start
  8.4 0.7 all-gather.7.cloned.1.call-update
  9.1 0.0 reduce-scatter.3.cloned.1.call-start
  9.1 1.0 slice.21
  10.2 0.8 reduce-window.8
  11.0 0.2 copy.48
  11.2 0.1 convert_reduce_fusion
  11.4 0.1 dynamic_slice.7
  11.4 3.8 fusion.6
  15.2 33.6 %all-gather.5.cloned.1.call-done = bf16[6144,1,256]{2,0,1:T(8,128)(2,1)} async-done(((bf16[384,1,256]{2,0,1:T(8,128)(2,1)}), bf16[6144,1,256]{2,0,1:T(8,128)(2,1)}) %all-gather.5.cloned.1.call-update) | async-done | bytes 3145744 | tf_op jit(solution)/shard_map/all_gather | solution.py:41
  48.8 5.4 %fusion = (f32[384,2]{0,1:T(2,128)S(1)}, f32[6144,384,2]{1,0,2:T(8,128)S(1)}) fusion(pred[384,6144]{0,1:T(8,128)(4,1)} %fusion.6, bf16[384,2,256]{0,2,1:T(8,128)(2,1)S(1)} %bitcast.102, bf16[6144,1,256]{2,0,1:T(8,128)(2,1)} %all-gather.5.cloned.1.call-done), kind=kOutput, calls=%fused_computation.2 | convolution fusion | flops 2430074112 | bytes 24775680 | tf_op jit(solution)/shard_map/qgrd,kgd->qgrk/dot_general | solution.py:54
  54.2 0.0 copy-start
  54.2 6.5 %copy-done = f32[6144,384,2]{1,0,2:T(8,128)} copy-done((f32[6144,384,2]{1,0,2:T(8,128)}, f32[6144,384,2]{1,0,2:T(8,128)S(1)}, u32[]{:S(2)}) %copy-start) | copy-done | bytes 18874392
  60.7 6.1 %fusion.1 = f32[384,2]{0,1:T(2,128)S(1)} fusion(f32[6144,384,2]{1,0,2:T(8,128)S(1)} %get-tuple-element.10, f32[384,2]{0,1:T(2,128)S(1)} %get-tuple-element.9, pred[384,6144]{0,1:T(8,128)(4,1)} %fusion.6), kind=kLoop, calls=%fused_computation.3 | loop fusion | flops 23592192 | bytes 21239808 | tf_op jit(solution)/shard_map/reduce_sum | solution.py:62
  66.8 19.6 %all-gather.7.cloned.1.call-done = bf16[6144,1,256]{2,0,1:T(8,128)(2,1)} async-done(((bf16[384,1,256]{2,0,1:T(8,128)(2,1)}), bf16[6144,1,256]{2,0,1:T(8,128)(2,1)}) %all-gather.7.cloned.1.call-update) | async-done | bytes 3145744 | tf_op jit(solution)/shard_map/all_gather | solution.py:42
  86.5 0.0 copy-start.2
  86.5 13.2 %fusion.32 = bf16[1,256,384,2]{2,1,3,0:T(8,128)(2,1)S(1)} fusion(bf16[6144,1,256]{2,0,1:T(8,128)(2,1)} %all-gather.7.cloned.1.call-done, f32[6144,384,2]{1,0,2:T(8,128)} %copy-done, f32[384,2]{0,1:T(2,128)S(1)} %get-tuple-element.9, pred[384,6144]{0,1:T(8,128)(4,1)} %fusion.6, f32[384,2]{0,1:T(2,128)S(1)} %fusion.1), kind=kOutput, calls=%fused_computation.33 | convolution fusion | flops 2439905280 | bytes 24778752 | tf_op jit(solution)/shard_map/qgrk,kgd->qgrd/dot_general | solution.py:63
  99.7 0.0 copy-done.2
  99.7 0.0 copy-start.3
  99.7 3.1 convolution_convert_fusion
  102.8 0.0 reduce-scatter.3.cloned.1.call-update
  102.8 0.2 all-gather.11.cloned.1.call-start
  103.1 0.0 copy-done.3
  103.1 0.5 copy.72
  103.6 6.2 %copy.53 = bf16[2,28,7168]{1,0,2:T(2,128)(2,1)} copy(bf16[2,28,7168]{2,1,0:T(8,128)(2,1)S(1)} %copy.72) | data formatting | bytes 1605632 | tf_op jit(solution)/shard_map/convert_element_type | solution.py:84
  109.7 8.3 %reshape.157 = bf16[8,2,25088]{2,1,0:T(2,128)(2,1)S(1)} reshape(bf16[7168,2,28]{2,1,0:T(2,128)(2,1)} %bitcast.96) | data formatting | bytes 1605632
  118.0 21.5 %all_to_all.23 = bf16[8,2,25088]{2,1,0:T(2,128)(2,1)S(1)} all-to-all(bf16[8,2,25088]{2,1,0:T(2,128)(2,1)S(1)} %reshape.157), channel_id=1, replica_groups=mesh['seq'=16,'tp'=8] {'tp'}, dimensions={0} | all-to-all | bytes 1605632 | tf_op jit(solution)/shard_map/all_to_all | solution.py:85
  139.5 10.6 %reshape.158 = bf16[7168,2,28]{2,1,0:T(2,128)(2,1)} reshape(bf16[8,2,25088]{2,1,0:T(2,128)(2,1)S(1)} %all_to_all.23) | data formatting | bytes 1605632
  150.1 0.0 copy-start.4
  150.1 0.0 copy-start.5
  150.1 0.0 copy-start.7
  150.1 9.9 %copy.54 = bf16[2,28,8,896]{3,0,1,2:T(2,128)(2,1)} copy(bf16[2,28,8,896]{1,0,3,2:T(2,128)(2,1)} %bitcast.97) | data formatting | bytes 1605632 | tf_op jit(solution)/shard_map/all_to_all | solution.py:85
  160.0 0.0 all-gather.11.cloned.1.call-update
  160.0 0.0 all-gather.9.cloned.1.call-start
  160.1 22.6 %reduce-scatter.3.cloned.1.call-done = bf16[48,3584]{1,0:T(8,128)(2,1)} async-done(((bf16[384,3584]{1,0:T(8,128)(2,1)}), bf16[48,3584]{1,0:T(8,128)(2,1)}) %reduce-scatter.3.cloned.1.call-update) | async-done | bytes 344080 | tf_op jit(solution)/shard_map/reduce_scatter | solution.py:76
  182.7 1.1 fusion.37
  183.8 0.0 copy-done.4
  183.8 0.0 copy-done.5
  183.9 1.3 multiply_reduce_fusion.1
  185.2 0.0 copy-done.7
  185.2 1.9 multiply_convert_fusion.1
  187.1 0.0 all-gather.9.cloned.1.call-update
  187.2 0.0 reduce-scatter.5.cloned.1.call-start
  187.2 70.7 %all-gather.11.cloned.1.call-done = bf16[2,3584,896]{2,0,1:T(2,128)(2,1)} async-done(((bf16[2,224,896]{2,0,1:T(2,128)(2,1)}), bf16[2,3584,896]{2,0,1:T(2,128)(2,1)}) %all-gather.11.cloned.1.call-update) | async-done | bytes 12845072 | tf_op jit(solution)/shard_map/all_gather | solution.py:86
  258.0 26.0 %fusion.46 = (bf16[1,3584,896]{2,0,1:T(2,128)(2,1)}, bf16[1,3584,896]{2,0,1:T(2,128)(2,1)}) fusion(bf16[2,3584,896]{2,0,1:T(2,128)(2,1)} %all-gather.11.cloned.1.call-done), kind=kLoop, calls=%fused_computation.58 | loop fusion | bytes 25690112 | tf_op jit(solution)/shard_map/slice | solution.py:87
  283.9 35.7 %all-gather.9.cloned.1.call-done = bf16[384,3584]{1,0:T(8,128)(2,1)} async-done(((bf16[48,3584]{1,0:T(8,128)(2,1)}), bf16[384,3584]{1,0:T(8,128)(2,1)}) %all-gather.9.cloned.1.call-update) | async-done | bytes 2752528 | tf_op jit(solution)/shard_map/all_gather | solution.py:83
  319.7 9.6 %fusion.9 = f32[384,896]{1,0:T(8,128)} fusion(bf16[384,3584]{1,0:T(8,128)(2,1)} %all-gather.9.cloned.1.call-done, bf16[1,3584,896]{2,0,1:T(2,128)(2,1)} %get-tuple-element.5), kind=kOutput, calls=%fused_computation.13 | convolution fusion | flops 2466250752 | bytes 10551296 | tf_op jit(solution)/shard_map/dot_general | solution.py:87
  329.3 0.0 copy-start.1
  329.3 0.0 copy-start.6
  329.3 15.2 %convolution_convert_fusion.1 = bf16[384,3584]{1,0:T(8,128)(2,1)} fusion(bf16[896,3584]{1,0:T(8,128)(2,1)} %param.16, bf16[384,3584]{1,0:T(8,128)(2,1)} %all-gather.9.cloned.1.call-done, bf16[1,3584,896]{2,0,1:T(2,128)(2,1)} %get-tuple-element.6, f32[384,896]{1,0:T(8,128)} %fusion.9), kind=kOutput, calls=%fused_computation.15 | convolution fusion | flops 4937318400 | bytes 19726336 | tf_op jit(solution)/shard_map/dot_general | solution.py:90
  344.5 0.0 reduce-scatter.5.cloned.1.call-update
  344.5 74.6 %reduce-scatter.5.cloned.1.call-done = bf16[48,3584]{1,0:T(8,128)(2,1)} async-done(((bf16[384,3584]{1,0:T(8,128)(2,1)}), bf16[48,3584]{1,0:T(8,128)(2,1)}) %reduce-scatter.5.cloned.1.call-update) | async-done | bytes 344080 | tf_op jit(solution)/shard_map/reduce_scatter | solution.py:76
  419.1 1.1 fusion.40
  420.2 0.0 copy-done.1
  420.2 0.0 copy-done.6
  420.3 1.4 multiply_reduce_fusion
  421.7 0.0 copy-done.8
  421.7 1.3 multiply_convert_fusion
  423.0 0.2 stack.2
  423.2 36.1 %all_to_all.24 = bf16[8,48,3584]{2,1,0:T(8,128)(2,1)S(1)} all-to-all(bf16[8,48,3584]{2,1,0:T(8,128)(2,1)S(1)} %stack.2), channel_id=1, replica_groups=mesh['seq'=16,'tp'=8] {'tp'}, dimensions={0} | all-to-all | bytes 5505024 | tf_op jit(solution)/shard_map/all_to_all | solution.py:94
  459.3 7.1 %convolution_convert_fusion.2 = bf16[384,1024]{1,0:T(8,128)(2,1)} fusion(bf16[384,3584]{1,0:T(8,128)(2,1)S(1)} %bitcast.99, bf16[3584,1024]{1,0:T(8,128)(2,1)} %param.17), kind=kOutput, calls=%fused_computation.22 | convolution fusion | flops 2818965504 | bytes 10878976 | tf_op jit(solution)/shard_map/dot_general | solution.py:96
  (6 shorter events, 0.0 us)
Async XLA Ops:
  6.5 42.2 %all-gather.5.cloned.1.call-start = ((), (), s32[]{:S(2)}) async-start(), calls=%async_computation.4 | async-start | bytes 3342336 | tf_op jit(solution)/shard_map/all_gather | solution.py:41
  8.3 78.1 %all-gather.7.cloned.1.call-start = ((), (), s32[]{:S(2)}) async-start(), calls=%async_computation.5 | async-start | bytes 3342336 | tf_op jit(solution)/shard_map/all_gather | solution.py:42
  9.1 173.6 %reduce-scatter.3.cloned.1.call-start = ((), (), s32[]{:S(2)}) async-start(), calls=%async_computation.6 | async-start | bytes 3096576 | tf_op jit(solution)/shard_map/reduce_scatter | solution.py:76
  54.2 6.5 %copy-start = (f32[6144,384,2]{1,0,2:T(8,128)}, f32[6144,384,2]{1,0,2:T(8,128)S(1)}, u32[]{:S(2)}) copy-start(f32[6144,384,2]{1,0,2:T(8,128)S(1)} %get-tuple-element.10) | copy-start | bytes 56623108
  86.5 13.2 %copy-start.2 = (bf16[512,3584]{1,0:T(8,128)(2,1)S(1)}, bf16[512,3584]{1,0:T(8,128)(2,1)}, u32[]{:S(2)}) copy-start(bf16[512,3584]{1,0:T(8,128)(2,1)} %param.14) | copy-start | bytes 11010052
  99.7 3.4 copy-start.3
  102.8 155.1 %all-gather.11.cloned.1.call-start = ((), (), s32[]{:S(2)}) async-start(), calls=%async_computation.8 | async-start | bytes 13647872 | tf_op jit(solution)/shard_map/all_gather | solution.py:86
  150.1 33.7 %copy-start.4 = (bf16[384,3584]{1,0:T(8,128)(2,1)S(1)}, bf16[384,3584]{1,0:T(8,128)(2,1)}, u32[]{:S(2)}) copy-start(bf16[384,3584]{1,0:T(8,128)(2,1)} %param.11) | copy-start | bytes 8257540
  150.1 33.7 %copy-start.5 = (f32[3584]{0:T(1024)S(1)}, f32[3584]{0:T(1024)}, u32[]{:S(2)}) copy-start(f32[3584]{0:T(1024)} %param.18) | copy-start | bytes 43012
  150.1 35.1 %copy-start.7 = (f32[3584]{0:T(1024)S(1)}, f32[3584]{0:T(1024)}, u32[]{:S(2)}) copy-start(f32[3584]{0:T(1024)} %param.19) | copy-start | bytes 43012
  160.0 159.7 %all-gather.9.cloned.1.call-start = ((), (), s32[]{:S(2)}) async-start(), calls=%async_computation.7 | async-start | bytes 3096576 | tf_op jit(solution)/shard_map/all_gather | solution.py:83
  187.2 231.9 %reduce-scatter.5.cloned.1.call-start = ((), (), s32[]{:S(2)}) async-start(), calls=%async_computation.9 | async-start | bytes 3096576 | tf_op jit(solution)/shard_map/reduce_scatter | solution.py:76
  329.3 91.0 %copy-start.1 = (bf16[48,3584]{1,0:T(8,128)(2,1)S(1)}, bf16[48,3584]{1,0:T(8,128)(2,1)}, u32[]{:S(2)}) copy-start(bf16[48,3584]{1,0:T(8,128)(2,1)} %reduce-scatter.3.cloned.1.call-done) | copy-start | bytes 1032196
  329.3 91.0 %copy-start.6 = (f32[3584]{0:T(1024)S(1)}, f32[3584]{0:T(1024)}, u32[]{:S(2)}) copy-start(f32[3584]{0:T(1024)} %param.20) | copy-start | bytes 43012
  344.5 77.2 %copy-start.8 = (f32[3584]{0:T(1024)S(1)}, f32[3584]{0:T(1024)}, u32[]{:S(2)}) copy-start(f32[3584]{0:T(1024)} %param.21) | copy-start | bytes 43012
Sparse Core Ops, SparseCore 0:
  9.1 39.6 all-gather.4
  50.5 35.9 all-gather.6
  103.0 79.6 reduce-scatter.2
  184.2 73.6 all-gather.10
  260.1 59.5 all-gather.8
  344.6 74.4 reduce-scatter.4
